TPU v7x, 32 devices: a whole 2x2x4 slice. The times are simulated.
32 devices in a mesh: dp: 8 (over z, y), tensor: 4 (over x, core).
Axes of the slice: x: 2, y: 2, z: 4, core: 2. Of those that a mesh axis runs over, the one named last changes fastest.
Arguments:
- hidden: bfloat16 [4096, 4096], P('dp'), may hold values from -40 to 40
- q_weight: bfloat16 [8192, 1024], P('dp', 'tensor'), may hold values from -0.09375 to 0.09375
- kv_weight: bfloat16 [8192, 512], P('dp', 'tensor'), may hold values from -0.09375 to 0.09375
- owner: int32 [4], replicated, may hold values from 0 to 1
- lengths: int32 [16], P('dp'), may hold values from 64 to 256, as said below
Outputs:
- attended: bfloat16 [4096, 1024], P('dp', 'tensor')
Inputs may be any that keep to these rules, and one draw needn't show every extreme that they name: `lengths`: some sequence has length exactly 256.
All inputs are finite; a program needn't handle non-finite values.
Results may differ from a plain program's by a relative error of at most 0.0092.
Values may be sent and summed in bfloat16 or wider, within the bound.
No kernel may reach another device: no remote copies, remote signals or barrier semaphores. Data moves between devices by JAX's collectives and lax.ppermute only.
A program may use at most 64 MiB of HBM per device.

v0:
```python
import math
import jax
import jax.numpy as jnp
from jax import lax
from jax.sharding import PartitionSpec as P

HEAD_DIM = 128
SEQ_LEN = 256
OLD_DATA = 4


def spread(value, axis, root):
    mine = lax.axis_index(axis) == root
    return lax.psum(jnp.where(mine, value, jnp.zeros_like(value)), axis)


def from_partner(value, axis, stride):
    mask = 2**stride
    pairs = [(source, source ^ mask) for source in range(lax.axis_size(axis))]
    return lax.ppermute(value, axis, pairs)


def rotate(values, positions, columns, active):
    pair_index = columns % HEAD_DIM // 2
    inverse = jnp.exp(-(2.0 * pair_index.astype(jnp.float32) / HEAD_DIM) * math.log(10000.0))
    angles = positions.astype(jnp.float32)[:, None] * inverse[None, :]
    signs = jnp.where(columns % 2 == 0, -1.0, 1.0).astype(jnp.float32)
    swapped = values.reshape(values.shape[0], -1, 2)[:, :, ::-1].reshape(values.shape)
    turned = values * jnp.cos(angles) + swapped * (jnp.sin(angles) * signs[None, :])
    return jnp.where(active[None, :], turned, values)


def body(hidden, q_weight, kv_weight, owner, lengths):
    row_count = hidden.shape[0]
    q_blocks = []
    kv_blocks = []
    for quarter in range(OLD_DATA):
        root_rank = owner[quarter] * OLD_DATA + quarter
        fetched_q, fetched_kv = (
            spread(q_weight, "dp", root_rank),
            spread(kv_weight, "dp", root_rank),
        )
        q_blocks.append(fetched_q)
        kv_blocks.append(fetched_kv)
    queries = jnp.dot(hidden, jnp.concatenate(q_blocks, axis=0), preferred_element_type=jnp.float32)
    keyvals = jnp.dot(
        hidden, jnp.concatenate(kv_blocks, axis=0), preferred_element_type=jnp.float32
    )
    positions = jnp.arange(row_count) % SEQ_LEN
    tensor_index = lax.axis_index("tensor")
    kv_width = kv_weight.shape[1]
    q_columns = jnp.arange(queries.shape[1])
    queries = rotate(queries, positions, q_columns, q_columns >= 0).astype(jnp.bfloat16)
    kv_columns = tensor_index * kv_width + jnp.arange(kv_width)
    keyvals = rotate(keyvals, positions, kv_columns, kv_columns // HEAD_DIM % 2 == 0).astype(
        jnp.bfloat16
    )
    partner = from_partner(keyvals, "tensor", 0)
    is_even = tensor_index % 2 == 0
    key_rows = jnp.where(is_even, keyvals, partner)
    value_rows = jnp.where(is_even, partner, keyvals)
    seq_count = row_count // SEQ_LEN
    per_device = queries.shape[1] // HEAD_DIM
    key_block = key_rows.reshape(seq_count, SEQ_LEN, HEAD_DIM)
    value_block = value_rows.reshape(seq_count, SEQ_LEN, HEAD_DIM)
    query_block = queries.reshape(seq_count, SEQ_LEN, per_device, HEAD_DIM)
    key_spots = jnp.arange(SEQ_LEN)
    allowed = (key_spots[None, None, :] <= key_spots[None, :, None]) & (
        key_spots[None, None, :] < lengths[:, None, None]
    )
    scores = jnp.einsum(
        "sqhd,skd->shqk", query_block, key_block, preferred_element_type=jnp.float32
    ) / math.sqrt(HEAD_DIM)
    scores = jnp.where(allowed[:, None, :, :], scores, -1e30)
    row_max = jnp.max(scores, axis=-1, keepdims=True)
    raised = jnp.exp(scores - row_max)
    row_total = jnp.sum(raised, axis=-1, keepdims=True)
    probs = (raised / row_total).astype(jnp.bfloat16)
    mixed = jnp.einsum("shqk,skd->sqhd", probs, value_block, preferred_element_type=jnp.float32)
    return mixed.astype(jnp.bfloat16).reshape(row_count, per_device * HEAD_DIM)


def solution(mesh):
    return jax.shard_map(
        body,
        mesh=mesh,
        in_specs=(P("dp", None), P("dp", "tensor"), P("dp", "tensor"), P(), P("dp")),
        out_specs=P("dp", "tensor"),
        check_vma=False,
    )
```

profile of v0, /device:TPU:0, one launch (start us, length us, event | category | flops | bytes accessed | tf_op | source)
XLA Modules:
  0.0 170.9 jit_solution(3968873753242986457)
XLA Ops:
  6.5 0.0 copy-start.4
  6.5 0.0 all-reduce.3.cloned.1.call-start
  6.5 1.5 fusion.51
  10.5 2.4 %broadcast_select_fusion.3 = (bf16[1024,256]{1,0:T(8,128)(2,1)}, bf16[1024,256]{1,0:T(8,128)(2,1)}, bf16[1024,256]{1,0:T(8,128)(2,1)}, bf16[1024,256]{1,0:T(8,128)(2,1)}) fusion(bf16[1024,256]{1,0:T(8,128)(2,1)} %param.6, pred[]{:T(512)S(6)} %eq.53, pred[]{:T(512)S(6)} %eq.54, pred[]{:T(512)S(6)} %eq.56, pred[]{:T(512)S(6)} %eq.55), kind=kLoop, calls=%fused_computation.36 | loop fusion | flops 1048576 | bytes 2621444 | tf_op jit(solution)/shard_map/jit(_where)/select_n | solution.py:14
  12.9 1.9 %broadcast_select_fusion.7 = (bf16[1024,128]{1,0:T(8,128)(2,1)}, bf16[1024,128]{1,0:T(8,128)(2,1)}, bf16[1024,128]{1,0:T(8,128)(2,1)}, bf16[1024,128]{1,0:T(8,128)(2,1)}) fusion(bf16[1024,128]{1,0:T(8,128)(2,1)} %param.7, pred[]{:T(512)S(6)} %eq.53, pred[]{:T(512)S(6)} %eq.54, pred[]{:T(512)S(6)} %eq.56, pred[]{:T(512)S(6)} %eq.55), kind=kLoop, calls=%fused_computation.52 | loop fusion | flops 524288 | bytes 1310724 | tf_op jit(solution)/shard_map/jit(_where)/select_n | solution.py:14
  14.8 0.0 all-reduce.3.cloned.1.call-update
  15.0 0.0 copy-done.4
  15.0 0.1 iota_compare_fusion.1
  15.1 0.1 broadcast_and_fusion
  15.2 131.7 %all-reduce.3.cloned.1.call-done = (bf16[1024,128]{1,0:T(8,128)(2,1)}, bf16[1024,128]{1,0:T(8,128)(2,1)}, bf16[1024,128]{1,0:T(8,128)(2,1)}, bf16[1024,128]{1,0:...) async-done(((bf16[1024,128]{1,0:T(8,128)(2,1)}, bf16[1024,128]{1,0:T(8,128)(2,1)}, ...) | async-done | bytes 3145744 | tf_op jit(solution)/shard_map/psum | solution.py:14
  146.9 0.0 copy-start
  146.9 0.0 copy-start.1
  146.9 0.0 copy-start.2
  146.9 0.0 copy-start.3
  146.9 4.2 %fusion.13 = f32[512,256]{0,1:T(8,128)S(1)} fusion(bf16[512,4096]{1,0:T(8,128)(2,1)} %param.5, bf16[1024,256]{1,0:T(8,128)(2,1)} %get-tuple-element.9, bf16[1024,256]{1,0:T(8,128)(2,1)} %get-tuple-element.10, bf16[1024,256]{1,0:T(8,128)(2,1)} %get-tuple-element.11, bf16[1024,256]{1,0:T(8,128)(2,1)} %get-tuple-element.12), kind=kOutput, calls=%fused_computation.14 | convolution fusion | flops 1082130432 | bytes 6815744 | tf_op jit(solution)/shard_map/dot_general | solution.py:45
  151.1 0.3 reshape.210
  151.4 1.4 rev.7
  152.8 0.4 reshape.211
  153.2 0.0 copy-done
  153.2 0.0 copy-done.1
  153.2 0.0 copy-done.2
  153.2 0.0 copy-done.3
  153.3 3.7 %convolution_bitcast_fusion = f32[512,128]{0,1:T(8,128)S(1)} fusion(bf16[512,4096]{1,0:T(8,128)(2,1)} %param.5, bf16[1024,128]{1,0:T(8,128)(2,1)S(1)} %copy-done, bf16[1024,128]{1,0:T(8,128)(2,1)S(1)} %copy-done.1, bf16[1024,128]{1,0:T(8,128)(2,1)S(1)} %copy-done.2, bf16[1024,128]{1,0:T(8,128)(2,1)S(1)} %copy-done.3), kind=kOutput, calls=%fused_computation.17 | convolution fusion | flops 541065216 | bytes 5505024 | tf_op jit(solution)/shard_map/dot_general | solution.py:46
  157.0 0.1 reshape.206
  157.1 0.7 rev.6
  157.9 0.2 reshape.207
  158.1 1.2 fusion.32
  159.3 0.1 collective-permute-start
  159.4 2.3 %fusion.26 = bf16[512,256]{0,1:T(8,128)(2,1)S(1)} fusion(f32[512,256]{0,1:T(8,128)S(1)} %fusion.13, f32[512,256]{0,1:T(8,128)S(1)} %reshape.211, f32[256]{0:T(256)S(1)} %get-tuple-element.29, f32[256]{0:T(256)S(1)} %get-tuple-element.30, f32[512]{0:T(512)S(1)} %fusion.39), kind=kLoop, calls=%fused_computation.30 | loop fusion | flops 786432 | bytes 1314816 | tf_op jit(solution)/shard_map/convert_element_type | solution.py:53
  161.7 0.1 reshape.212
  161.7 0.0 collective-permute-done
  161.8 0.1 copy.20
  161.9 0.3 fusion.12
  162.2 0.5 fusion.52
  162.7 0.4 fusion.16
  163.2 0.2 copy.14
  163.3 0.7 copy.31
  (7 shorter events, 0.1 us)
Async XLA Ops:
  6.5 8.4 %copy-start.4 = (s32[2]{0:T(128)S(1)}, s32[2]{0:T(128)}, u32[]{:S(2)}) copy-start(s32[2]{0:T(128)} %param.9) | copy-start | bytes 28
  6.5 140.4 %all-reduce.3.cloned.1.call-start = ((), (), s32[]{:S(2)}) async-start(), calls=%async_computation | async-start | bytes 6291456 | tf_op jit(solution)/shard_map/psum | solution.py:14
  146.9 6.3 %copy-start = (bf16[1024,128]{1,0:T(8,128)(2,1)S(1)}, bf16[1024,128]{1,0:T(8,128)(2,1)}, u32[]{:S(2)}) copy-start(bf16[1024,128]{1,0:T(8,128)(2,1)} %get-tuple-element.5) | copy-start | bytes 786436
  146.9 6.3 %copy-start.1 = (bf16[1024,128]{1,0:T(8,128)(2,1)S(1)}, bf16[1024,128]{1,0:T(8,128)(2,1)}, u32[]{:S(2)}) copy-start(bf16[1024,128]{1,0:T(8,128)(2,1)} %get-tuple-element.6) | copy-start | bytes 786436
  146.9 6.3 %copy-start.2 = (bf16[1024,128]{1,0:T(8,128)(2,1)S(1)}, bf16[1024,128]{1,0:T(8,128)(2,1)}, u32[]{:S(2)}) copy-start(bf16[1024,128]{1,0:T(8,128)(2,1)} %get-tuple-element.7) | copy-start | bytes 786436
  146.9 6.3 %copy-start.3 = (bf16[1024,128]{1,0:T(8,128)(2,1)S(1)}, bf16[1024,128]{1,0:T(8,128)(2,1)}, u32[]{:S(2)}) copy-start(bf16[1024,128]{1,0:T(8,128)(2,1)} %get-tuple-element.8) | copy-start | bytes 786436
  159.3 2.5 %collective-permute-start = (bf16[512,128]{0,1:T(8,128)(2,1)S(1)}, bf16[512,128]{0,1:T(8,128)(2,1)S(1)}, u32[]{:S(2)}, u32[]{:S(2)}) collective-permute-start(bf16[512,128]{0,1:T(8,128)(2,1)S(1)} %fusion.32), channel_id=1, source_target_pairs={{0,1},{1,0},{2,3},{3,2},{4,5},{5,4},{6,7},{7,6},{8,9},{9,8},{10,11... | collective-permute-start | bytes 393224 | tf_op jit(solution)/shard_map/ppermute | solution.py:20
Sparse Core Ops, SparseCore 0:
  15.0 131.8 all-reduce.2
where the time goes:
time: 171 us
  waiting for transfers between devices  132 us (77%)
  between operations  16.1 us (9%)
  matrix products  9.1 us (5%)
  other arithmetic  8.17 us (5%)
  local copies, waits for them, and re-layouts  5.75 us (3%)
    psum x1, waiting for transfers between devices, spread(): return lax.psum(jnp.where(mine, value, jnp.zeros_like(value)), axis)  132 us
    select_n x2, other arithmetic, spread(): return lax.psum(jnp.where(mine, value, jnp.zeros_like(value)), axis)  4.34 us
    dot_general x1, matrix products, body(): jnp.dot(hidden, jnp.concatenate(q_blocks, axis=0), preferred_element_type...  4.2 us
    dot_general x1, matrix products, body(): jnp.dot(hidden, jnp.concatenate(kv_blocks, axis=0), preferred_element_typ...  3.72 us
  transfers between devices with their start and end apart: 2, of which 1 were waited for; matrix products, arithmetic and copies ran while one was open for 2% of the time, Pallas kernels for 0%

commit v1 on v0

--- a/solution.py
+++ b/solution.py
@@ -11,7 +11,7 @@
 
 def spread(value, axis, root):
     mine = lax.axis_index(axis) == root
-    return lax.psum(jnp.where(mine, value, jnp.zeros_like(value)), axis)
+    return jnp.sum(lax.all_gather(jnp.where(mine, value, jnp.zeros_like(value)), axis), axis=0)
 
 
 def from_partner(value, axis, stride):

time: 171 us -> 528 us (3.09)
  waiting for transfers between devices: 132 us -> 468 us
  other arithmetic: 8.17 us -> 28.3 us
    all_gather x0 -> x8, waiting for transfers between devices: none -> 463 us  [spread(): lax.all_gather(jnp.where(mine, value, jnp.zeros_like(value)), axis)]
    psum x1 -> x0, waiting for transfers between devices: 132 us -> none  [spread(): return lax.psum(jnp.where(mine, value, jnp.zeros_like(value)), axis)]
    reduce_sum x0 -> x8, other arithmetic: none -> 20.1 us  [spread(): jnp.sum(lax.all_gather(jnp.where(mine, value, jnp.zeros_like(value)), axi...]
  transfers between devices with their start and end apart: 2 -> 9, of which waited for: 1 -> 9; matrix products, arithmetic and copies ran while one was open for 2% -> 5% of each run, Pallas kernels for 0% -> 0%
where the time goes in v1:
time: 528 us; the launch traced here: 527 us
  waiting for transfers between devices  468 us (89%)
  other arithmetic  28.3 us (5%)
  between operations  16.3 us (3%)
  matrix products  8.36 us (2%)
  local copies, waits for them, and re-layouts  5.75 us (1%)
    all_gather x8, waiting for transfers between devices, spread(): lax.all_gather(jnp.where(mine, value, jnp.zeros_like(value)), axis)  463 us
    reduce_sum x8, other arithmetic, spread(): jnp.sum(lax.all_gather(jnp.where(mine, value, jnp.zeros_like(value)), axi...  20.1 us
  transfers between devices with their start and end apart: 9, of which 9 were waited for; matrix products, arithmetic and copies ran while one was open for 5% of the time, Pallas kernels for 0%

profile of v1, /device:TPU:0, one launch (start us, length us, event | category | flops | bytes accessed | tf_op | source)
XLA Modules:
  0.0 527.3 jit_solution(12088580333871550815)
XLA Ops:
  6.5 1.5 fusion.51
  10.6 1.9 broadcast_select_fusion.7
  12.5 0.0 all-gather.19.cloned.1.call-start
  12.6 0.7 all-gather.19.cloned.1.call-update
  13.3 0.7 all-gather.21.cloned.1.call-update
  14.1 0.5 all-gather.23.cloned.1.call-update
  14.6 2.5 broadcast_select_fusion.3
  17.2 0.0 all-gather.27.cloned.1.call-start
  17.2 0.5 all-gather.27.cloned.1.call-update
  17.8 0.7 all-gather.29.cloned.1.call-update
  18.5 0.7 all-gather.31.cloned.1.call-update
  19.3 0.1 iota_compare_fusion.1
  19.4 45.1 %all-gather.17.cloned.1.call-done = bf16[8192,128]{1,0:T(8,128)(2,1)} async-done(((bf16[1024,128]{1,0:T(8,128)(2,1)}), bf16[8192,128]{1,0:T(8,128)(2,1)}) %all-gather.17.cloned.1.call-update) | async-done | bytes 2097168 | tf_op jit(solution)/shard_map/all_gather | solution.py:14
  64.5 2.0 reduce_sum.105
  66.5 47.8 %all-gather.19.cloned.1.call-done = bf16[8192,128]{1,0:T(8,128)(2,1)} async-done(((bf16[1024,128]{1,0:T(8,128)(2,1)}), bf16[8192,128]{1,0:T(8,128)(2,1)}) %all-gather.19.cloned.1.call-update) | async-done | bytes 2097168 | tf_op jit(solution)/shard_map/all_gather | solution.py:14
  114.3 2.0 reduce_sum.106
  116.3 47.8 %all-gather.21.cloned.1.call-done = bf16[8192,128]{1,0:T(8,128)(2,1)} async-done(((bf16[1024,128]{1,0:T(8,128)(2,1)}), bf16[8192,128]{1,0:T(8,128)(2,1)}) %all-gather.21.cloned.1.call-update) | async-done | bytes 2097168 | tf_op jit(solution)/shard_map/all_gather | solution.py:14
  164.1 2.0 reduce_sum.107
  166.0 47.7 %all-gather.23.cloned.1.call-done = bf16[8192,128]{1,0:T(8,128)(2,1)} async-done(((bf16[1024,128]{1,0:T(8,128)(2,1)}), bf16[8192,128]{1,0:T(8,128)(2,1)}) %all-gather.23.cloned.1.call-update) | async-done | bytes 2097168 | tf_op jit(solution)/shard_map/all_gather | solution.py:14
  213.7 2.0 reduce_sum.108
  215.7 3.7 convolution_bitcast_fusion
  219.4 0.1 reshape.206
  219.5 0.7 rev.6
  220.3 0.2 reshape.207
  220.5 1.2 fusion.32
  221.7 0.1 collective-permute-start
  221.8 0.1 broadcast_and_fusion
  221.9 1.2 collective-permute-done
  223.1 0.1 copy.20
  223.3 63.7 %all-gather.25.cloned.1.call-done = bf16[8192,256]{1,0:T(8,128)(2,1)} async-done(((bf16[1024,256]{1,0:T(8,128)(2,1)}), bf16[8192,256]{1,0:T(8,128)(2,1)}) %all-gather.25.cloned.1.call-update) | async-done | bytes 4194320 | tf_op jit(solution)/shard_map/all_gather | solution.py:14
  287.0 3.0 reduce_sum.109
  290.1 70.3 %all-gather.27.cloned.1.call-done = bf16[8192,256]{1,0:T(8,128)(2,1)} async-done(((bf16[1024,256]{1,0:T(8,128)(2,1)}), bf16[8192,256]{1,0:T(8,128)(2,1)}) %all-gather.27.cloned.1.call-update) | async-done | bytes 4194320 | tf_op jit(solution)/shard_map/all_gather | solution.py:14
  360.4 3.0 reduce_sum.110
  363.4 70.4 %all-gather.29.cloned.1.call-done = bf16[8192,256]{1,0:T(8,128)(2,1)} async-done(((bf16[1024,256]{1,0:T(8,128)(2,1)}), bf16[8192,256]{1,0:T(8,128)(2,1)}) %all-gather.29.cloned.1.call-update) | async-done | bytes 4194320 | tf_op jit(solution)/shard_map/all_gather | solution.py:14
  433.8 3.0 reduce_sum.111
  436.9 70.4 %all-gather.31.cloned.1.call-done = bf16[8192,256]{1,0:T(8,128)(2,1)} async-done(((bf16[1024,256]{1,0:T(8,128)(2,1)}), bf16[8192,256]{1,0:T(8,128)(2,1)}) %all-gather.31.cloned.1.call-update) | async-done | bytes 4194320 | tf_op jit(solution)/shard_map/all_gather | solution.py:14
  507.3 3.0 reduce_sum.112
  510.4 3.5 fusion.13
  513.9 0.3 reshape.210
  514.2 1.4 rev.7
  515.6 0.4 reshape.211
  516.0 2.3 fusion.26
  518.3 0.1 reshape.212
  518.4 0.3 fusion.12
  518.7 0.5 fusion.52
  519.1 0.4 fusion.16
  519.6 0.2 copy.14
  519.7 0.7 copy.31
  (17 shorter events, 0.4 us)
Async XLA Ops:
  6.5 12.8 %copy-start = (s32[2]{0:T(128)S(1)}, s32[2]{0:T(128)}, u32[]{:S(2)}) copy-start(s32[2]{0:T(128)} %param.9) | copy-start | bytes 28
  6.5 58.0 %all-gather.17.cloned.1.call-start = ((), (), s32[]{:S(2)}) async-start(), calls=%async_computation | async-start | bytes 2359296 | tf_op jit(solution)/shard_map/all_gather | solution.py:14
  12.5 101.7 %all-gather.19.cloned.1.call-start = ((), (), s32[]{:S(2)}) async-start(), calls=%async_computation.1 | async-start | bytes 2359296 | tf_op jit(solution)/shard_map/all_gather | solution.py:14
  13.3 150.8 %all-gather.21.cloned.1.call-start = ((), (), s32[]{:S(2)}) async-start(), calls=%async_computation.2 | async-start | bytes 2359296 | tf_op jit(solution)/shard_map/all_gather | solution.py:14
  14.0 199.7 %all-gather.23.cloned.1.call-start = ((), (), s32[]{:S(2)}) async-start(), calls=%async_computation.3 | async-start | bytes 2359296 | tf_op jit(solution)/shard_map/all_gather | solution.py:14
  14.6 272.4 %all-gather.25.cloned.1.call-start = ((), (), s32[]{:S(2)}) async-start(), calls=%async_computation.4 | async-start | bytes 4718592 | tf_op jit(solution)/shard_map/all_gather | solution.py:14
  17.2 343.2 %all-gather.27.cloned.1.call-start = ((), (), s32[]{:S(2)}) async-start(), calls=%async_computation.5 | async-start | bytes 4718592 | tf_op jit(solution)/shard_map/all_gather | solution.py:14
  17.7 416.1 %all-gather.29.cloned.1.call-start = ((), (), s32[]{:S(2)}) async-start(), calls=%async_computation.6 | async-start | bytes 4718592 | tf_op jit(solution)/shard_map/all_gather | solution.py:14
  18.5 488.8 %all-gather.31.cloned.1.call-start = ((), (), s32[]{:S(2)}) async-start(), calls=%async_computation.7 | async-start | bytes 4718592 | tf_op jit(solution)/shard_map/all_gather | solution.py:14
  221.7 1.4 collective-permute-start
Sparse Core Ops, SparseCore 0:
  12.7 51.7 all-gather.16
  66.6 47.6 all-gather.18
  116.4 47.6 all-gather.20
  166.0 47.6 all-gather.22
  215.7 71.3 all-gather.24
  289.0 71.3 all-gather.26
  362.5 71.3 all-gather.28
  436.0 71.3 all-gather.30
